TPU v7x, 32 devices: a whole 2x2x4 slice. The times are simulated.
32 devices in a mesh: ctx: 8 (over z, y), fsdp: 4 (over x, core).
Axes of the slice: x: 2, y: 2, z: 4, core: 2. Of those that a mesh axis runs over, the one named last changes fastest.
Arguments:
- tokens: bfloat16 [4, 2048, 1024], P('fsdp', 'ctx'), may hold values from -6 to 6
- out_grad: bfloat16 [4, 2048, 1024], P('fsdp', 'ctx'), may hold values from -6 to 6
- lengths: int32 [4, 1], P('fsdp'), may hold values from 512 to 2048, as said below
- norm1_gain: bfloat16 [1024], P('fsdp'), may hold values from 0.5 to 1.5
- w_query: bfloat16 [1024, 1024], P('fsdp'), may hold values from -0.1875 to 0.1875
- w_latent: bfloat16 [1024, 512], P('fsdp'), may hold values from -0.1875 to 0.1875
- w_key_up: bfloat16 [1024, 256], P('fsdp'), may hold values from -0.75 to 0.75
- w_value_up: bfloat16 [1024, 256], P('fsdp'), may hold values from -0.375 to 0.375
- w_output: bfloat16 [1024, 1024], P('fsdp'), may hold values from -1.5 to 1.5
- norm2_gain: bfloat16 [1024], P('fsdp'), may hold values from 0.5 to 1.5
- w_gate: bfloat16 [1024, 2816], P(None, 'fsdp'), may hold values from -0.1875 to 0.1875
- w_up: bfloat16 [1024, 2816], P(None, 'fsdp'), may hold values from -0.1875 to 0.1875
- w_down: bfloat16 [2816, 1024], P('fsdp'), may hold values from -0.109375 to 0.109375
Outputs:
- result: bfloat16 [4, 2048, 1024], P('fsdp', 'ctx')
- token_grad: float32 [4, 2048, 1024], P('fsdp', 'ctx')
- norm1_gain_grad: float32 [1024], P('fsdp')
- w_query_grad: float32 [1024, 1024], P('fsdp')
- w_latent_grad: float32 [1024, 512], P('fsdp')
- w_key_up_grad: float32 [1024, 256], P('fsdp')
- w_value_up_grad: float32 [1024, 256], P('fsdp')
- w_output_grad: float32 [1024, 1024], P('fsdp')
- norm2_gain_grad: float32 [1024], P('fsdp')
- w_gate_grad: float32 [1024, 2816], P(None, 'fsdp')
- w_up_grad: float32 [1024, 2816], P(None, 'fsdp')
- w_down_grad: float32 [2816, 1024], P('fsdp')
Inputs may be any that keep to these rules, and one draw needn't show every extreme that they name: lengths[g, j] valid tokens stand at the start of slot j of group g; the rest of the slot of 2048 rows is padding.
All inputs are finite; a program needn't handle non-finite values.
Results may differ from a plain program's by a relative error of at most 0.025.
Values may be sent and summed in bfloat16 or wider, within the bound.
No kernel may reach another device: no remote copies, remote signals or barrier semaphores. Data moves between devices by JAX's collectives and lax.ppermute only.
A program may use at most 192 MiB of HBM per device.

v0:
```python
import jax
import jax.numpy as jnp
from jax import lax
from jax.sharding import PartitionSpec as P

NH = 16
HD = 64
LAT = 256
GRP = 2
SEQ_MAX = 4096
EPS = 1e-06
NEGATIVE = -1e30


def norm_scale(values):
    return lax.rsqrt(jnp.mean(values * values, axis=-1, keepdims=True) + EPS)


def norm_back(grad_in, normed, scale_rows, gain_full):
    scaled = grad_in * gain_full
    return scale_rows * (scaled - normed * jnp.mean(scaled * normed, axis=-1, keepdims=True))


def key_mask(key_start, key_rows, slot_start, query_pos, length):
    relative = key_start - slot_start + jnp.arange(key_rows, dtype=jnp.int32)
    return (
        (relative[None, :] >= 0)
        & (relative[None, :] <= query_pos[:, None])
        & (relative[None, :] < length)
    )


def raw_scores(query_groups, key_piece, allowed, score_scale):
    grouped = key_piece.reshape(key_piece.shape[0], GRP, LAT)
    scores = (
        jnp.einsum("gpql,kgl->gpqk", query_groups, grouped, preferred_element_type=jnp.float32)
        * score_scale
    )
    return (jnp.where(allowed[None, None], scores, NEGATIVE), grouped)


def on_device(
    tokens,
    out_grad,
    lengths,
    norm1_gain,
    w_query,
    w_latent,
    w_key_up,
    w_value_up,
    w_output,
    norm2_gain,
    w_gate,
    w_up,
    w_down,
):
    ctx_size = lax.axis_size("ctx")
    tok_rows = tokens.shape[1]
    group_rows = tok_rows * ctx_size
    seq_rows = min(SEQ_MAX, group_rows)
    slot_blocks = seq_rows // tok_rows
    head_groups = NH // GRP
    lat_width = GRP * LAT
    my_start = lax.axis_index("ctx") * tok_rows
    slot_number = my_start // seq_rows
    slot_start = slot_number * seq_rows
    length = jnp.sum(
        jnp.where(jnp.arange(lengths.shape[1], dtype=jnp.int32) == slot_number, lengths[0], 0)
    )
    query_pos = my_start - slot_start + jnp.arange(tok_rows, dtype=jnp.int32)
    row_valid = (query_pos < length).astype(jnp.float32)[:, None]
    score_scale = HD ** (-0.5)
    gain_one, query_full, latent_full, key_full, value_full, output_full = (
        lax.all_gather(norm1_gain, "fsdp", axis=0, tiled=True),
        lax.all_gather(w_query, "fsdp", axis=0, tiled=True),
        lax.all_gather(w_latent, "fsdp", axis=0, tiled=True),
        lax.all_gather(w_key_up, "fsdp", axis=0, tiled=True),
        lax.all_gather(w_value_up, "fsdp", axis=0, tiled=True),
        lax.all_gather(w_output, "fsdp", axis=0, tiled=True),
    )
    gain_two, gate_full, up_full, down_full = (
        lax.all_gather(norm2_gain, "fsdp", axis=0, tiled=True),
        lax.all_gather(w_gate, "fsdp", axis=1, tiled=True),
        lax.all_gather(w_up, "fsdp", axis=1, tiled=True),
        lax.all_gather(w_down, "fsdp", axis=0, tiled=True),
    )
    gain_one_f = gain_one.astype(jnp.float32)
    gain_two_f = gain_two.astype(jnp.float32)
    inputs = tokens[0].astype(jnp.float32)
    scale_one = norm_scale(inputs)
    normed_one = inputs * scale_one
    normed = (normed_one * gain_one_f).astype(jnp.bfloat16)
    queries = jnp.dot(normed, query_full, preferred_element_type=jnp.float32).astype(jnp.bfloat16)
    latent = jnp.dot(normed, latent_full, preferred_element_type=jnp.float32).astype(jnp.bfloat16)
    key_heads = key_full.reshape(NH, HD, LAT)
    query_latent = jnp.einsum(
        "shd,hdl->hsl",
        queries.reshape(tok_rows, NH, HD),
        key_heads,
        preferred_element_type=jnp.float32,
    ).astype(jnp.bfloat16)
    query_groups = query_latent.reshape(GRP, head_groups, tok_rows, LAT)

    def is_needed(key_start, key_rows):
        return (
            (key_start + key_rows > slot_start)
            & (key_start < slot_start + length)
            & (key_start < my_start + tok_rows)
        )

    def forward_update(state_now, key_piece, key_start):
        best_now, weight_sum, accum_now = state_now
        allowed = key_mask(key_start, key_piece.shape[0], slot_start, query_pos, length)
        scores, grouped = raw_scores(query_groups, key_piece, allowed, score_scale)
        best_next = jnp.maximum(best_now, jnp.max(scores, axis=-1))
        factor = jnp.exp(best_now - best_next)
        weights = jnp.where(allowed[None, None], jnp.exp(scores - best_next[..., None]), 0.0)
        weight_sum = weight_sum * factor + jnp.sum(weights, axis=-1)
        accum_now = accum_now * factor[..., None] + jnp.einsum(
            "gpqk,kgl->gpql",
            weights.astype(jnp.bfloat16),
            grouped,
            preferred_element_type=jnp.float32,
        )
        return (best_next, weight_sum, accum_now)

    def guarded_forward(state_now, key_piece, key_start):
        return lax.cond(
            is_needed(key_start, key_piece.shape[0]),
            lambda state_in: forward_update(state_in, key_piece, key_start),
            lambda state_in: state_in,
            state_now,
        )

    start_state = (
        jnp.full((GRP, head_groups, tok_rows), NEGATIVE, jnp.float32),
        jnp.zeros((GRP, head_groups, tok_rows), jnp.float32),
        jnp.zeros((GRP, head_groups, tok_rows, LAT), jnp.float32),
    )
    group_latent = lax.all_gather(latent, "ctx", axis=0, tiled=True)

    def forward_loop(block_index, state_now):
        key_start = slot_start + block_index * tok_rows
        key_piece = lax.dynamic_slice_in_dim(group_latent, key_start, tok_rows, 0)
        return guarded_forward(state_now, key_piece, key_start)

    final_state = lax.fori_loop(0, slot_blocks, forward_loop, start_state)
    best_final, sum_final, accum_final = final_state
    log_total = best_final + jnp.log(sum_final)
    mixture = accum_final / sum_final[..., None]
    mixture_low = mixture.astype(jnp.bfloat16)
    value_heads = value_full.reshape(NH, HD, LAT)
    attended = (
        jnp.einsum(
            "hsl,hdl->shd",
            mixture_low.reshape(NH, tok_rows, LAT),
            value_heads,
            preferred_element_type=jnp.float32,
        )
        .reshape(tok_rows, NH * HD)
        .astype(jnp.bfloat16)
    )
    branch = jnp.dot(attended, output_full, preferred_element_type=jnp.float32)
    middle = inputs + branch
    scale_two = norm_scale(middle)
    normed_two_raw = middle * scale_two
    normed_two = (normed_two_raw * gain_two_f).astype(jnp.bfloat16)
    gate_value = jnp.dot(normed_two, gate_full, preferred_element_type=jnp.float32)
    upward = jnp.dot(normed_two, up_full, preferred_element_type=jnp.float32)
    sigmoid_gate = jax.nn.sigmoid(gate_value)
    silu_gate = gate_value * sigmoid_gate
    hidden = (silu_gate * upward).astype(jnp.bfloat16)
    feed_out = jnp.dot(hidden, down_full, preferred_element_type=jnp.float32)
    result = ((middle + feed_out) * row_valid).astype(jnp.bfloat16)
    cotangent = out_grad[0].astype(jnp.float32) * row_valid
    feed_grad = cotangent.astype(jnp.bfloat16)
    down_grad = jnp.einsum("tf,td->fd", hidden, feed_grad, preferred_element_type=jnp.float32)
    hidden_grad = jnp.einsum("td,fd->tf", feed_grad, down_full, preferred_element_type=jnp.float32)
    gate_grad = (
        hidden_grad * upward * sigmoid_gate * (1.0 + gate_value * (1.0 - sigmoid_gate))
    ).astype(jnp.bfloat16)
    up_grad_in = (hidden_grad * silu_gate).astype(jnp.bfloat16)
    gate_w_grad = jnp.einsum("td,tf->df", normed_two, gate_grad, preferred_element_type=jnp.float32)
    up_w_grad = jnp.einsum("td,tf->df", normed_two, up_grad_in, preferred_element_type=jnp.float32)
    normed_two_grad = jnp.einsum(
        "tf,df->td", gate_grad, gate_full, preferred_element_type=jnp.float32
    ) + jnp.einsum("tf,df->td", up_grad_in, up_full, preferred_element_type=jnp.float32)
    gain_two_grad = jnp.sum(normed_two_grad * normed_two_raw, axis=0)
    middle_grad = cotangent + norm_back(normed_two_grad, normed_two_raw, scale_two, gain_two_f)
    branch_grad = middle_grad.astype(jnp.bfloat16)
    output_grad = jnp.einsum("tk,td->kd", attended, branch_grad, preferred_element_type=jnp.float32)
    attended_grad = jnp.einsum(
        "td,kd->tk", branch_grad, output_full, preferred_element_type=jnp.float32
    ).astype(jnp.bfloat16)
    attended_heads = attended_grad.reshape(tok_rows, NH, HD)
    value_grad = jnp.einsum(
        "shd,hsl->hdl",
        attended_heads,
        mixture_low.reshape(NH, tok_rows, LAT),
        preferred_element_type=jnp.float32,
    ).reshape(NH * HD, LAT)
    mixture_grad = (
        jnp.einsum("shd,hdl->hsl", attended_heads, value_heads, preferred_element_type=jnp.float32)
        .astype(jnp.bfloat16)
        .reshape(GRP, head_groups, tok_rows, LAT)
    )
    delta_sum = jnp.sum(mixture_grad * mixture, axis=-1)

    def back_term(query_grad_sum, key_piece, key_start):

        def compute(sum_in):
            allowed = key_mask(key_start, tok_rows, slot_start, query_pos, length)
            scores, grouped = raw_scores(query_groups, key_piece, allowed, score_scale)
            probs = jnp.where(allowed[None, None], jnp.exp(scores - log_total[..., None]), 0.0)
            probs_low = probs.astype(jnp.bfloat16)
            prob_grad = jnp.einsum(
                "gpql,kgl->gpqk", mixture_grad, grouped, preferred_element_type=jnp.float32
            )
            score_grad = (probs * (prob_grad - delta_sum[..., None])).astype(jnp.bfloat16)
            sum_out = sum_in + score_scale * jnp.einsum(
                "gpqk,kgl->gpql", score_grad, grouped, preferred_element_type=jnp.float32
            )
            key_term = score_scale * jnp.einsum(
                "gpqk,gpql->kgl", score_grad, query_groups, preferred_element_type=jnp.float32
            ) + jnp.einsum(
                "gpqk,gpql->kgl", probs_low, mixture_grad, preferred_element_type=jnp.float32
            )
            return (sum_out, key_term.reshape(tok_rows, lat_width))

        def skipped(sum_in):
            return (sum_in, jnp.zeros((tok_rows, lat_width), jnp.float32))

        return lax.cond(is_needed(key_start, tok_rows), compute, skipped, query_grad_sum)

    zero_query = jnp.zeros((GRP, head_groups, tok_rows, LAT), jnp.float32)

    def backward_loop(block_index, state_now):
        sum_now, key_grads = state_now
        key_start = slot_start + block_index * tok_rows
        key_piece = lax.dynamic_slice_in_dim(group_latent, key_start, tok_rows, 0)
        sum_now, key_term = back_term(sum_now, key_piece, key_start)
        key_grads = lax.dynamic_update_slice_in_dim(key_grads, key_term, block_index * tok_rows, 0)
        return (sum_now, key_grads)

    back_start = (zero_query, jnp.zeros((seq_rows, lat_width), jnp.float32))
    query_lat_grad, slot_key_grads = lax.fori_loop(0, slot_blocks, backward_loop, back_start)
    row_count = tok_rows * lax.axis_size("ctx")
    padding = jnp.zeros((row_count, lat_width), jnp.float32)
    padded = jnp.concatenate([padding, slot_key_grads, padding], axis=0)
    offset = jnp.clip(jnp.int32(0) - slot_start + row_count, 0, seq_rows + row_count)
    latent_grad = lax.psum_scatter(
        lax.dynamic_slice_in_dim(padded, offset, row_count, 0).astype(jnp.bfloat16),
        "ctx",
        scatter_dimension=0,
        tiled=True,
    )
    query_lat_low = query_lat_grad.reshape(NH, tok_rows, LAT).astype(jnp.bfloat16)
    key_up_grad = jnp.einsum(
        "shd,hsl->hdl",
        queries.reshape(tok_rows, NH, HD),
        query_lat_low,
        preferred_element_type=jnp.float32,
    ).reshape(NH * HD, LAT)
    query_grad = (
        jnp.einsum("hsl,hdl->shd", query_lat_low, key_heads, preferred_element_type=jnp.float32)
        .reshape(tok_rows, NH * HD)
        .astype(jnp.bfloat16)
    )
    query_w_grad = jnp.einsum("td,tk->dk", normed, query_grad, preferred_element_type=jnp.float32)
    latent_w_grad = jnp.einsum("td,tk->dk", normed, latent_grad, preferred_element_type=jnp.float32)
    normed_grad = jnp.einsum(
        "tk,dk->td", query_grad, query_full, preferred_element_type=jnp.float32
    ) + jnp.einsum("tk,dk->td", latent_grad, latent_full, preferred_element_type=jnp.float32)
    gain_one_grad = jnp.sum(normed_grad * normed_one, axis=0)
    input_grad = middle_grad + norm_back(normed_grad, normed_one, scale_one, gain_one_f)
    shards = (
        lax.psum_scatter(
            gain_one_grad.astype(jnp.bfloat16), "fsdp", scatter_dimension=0, tiled=True
        ).astype(jnp.float32),
        lax.psum_scatter(
            query_w_grad.astype(jnp.bfloat16), "fsdp", scatter_dimension=0, tiled=True
        ).astype(jnp.float32),
        lax.psum_scatter(
            latent_w_grad.astype(jnp.bfloat16), "fsdp", scatter_dimension=0, tiled=True
        ).astype(jnp.float32),
        lax.psum_scatter(
            key_up_grad.astype(jnp.bfloat16), "fsdp", scatter_dimension=0, tiled=True
        ).astype(jnp.float32),
        lax.psum_scatter(
            value_grad.astype(jnp.bfloat16), "fsdp", scatter_dimension=0, tiled=True
        ).astype(jnp.float32),
        lax.psum_scatter(
            output_grad.astype(jnp.bfloat16), "fsdp", scatter_dimension=0, tiled=True
        ).astype(jnp.float32),
        lax.psum_scatter(
            gain_two_grad.astype(jnp.bfloat16), "fsdp", scatter_dimension=0, tiled=True
        ).astype(jnp.float32),
        lax.psum_scatter(
            gate_w_grad.astype(jnp.bfloat16), "fsdp", scatter_dimension=1, tiled=True
        ).astype(jnp.float32),
        lax.psum_scatter(
            up_w_grad.astype(jnp.bfloat16), "fsdp", scatter_dimension=1, tiled=True
        ).astype(jnp.float32),
        lax.psum_scatter(
            down_grad.astype(jnp.bfloat16), "fsdp", scatter_dimension=0, tiled=True
        ).astype(jnp.float32),
    )
    summed = (
        lax.psum(shards[0].astype(jnp.bfloat16), "ctx").astype(jnp.float32),
        lax.psum(shards[1].astype(jnp.bfloat16), "ctx").astype(jnp.float32),
        lax.psum(shards[2].astype(jnp.bfloat16), "ctx").astype(jnp.float32),
        lax.psum(shards[3].astype(jnp.bfloat16), "ctx").astype(jnp.float32),
        lax.psum(shards[4].astype(jnp.bfloat16), "ctx").astype(jnp.float32),
        lax.psum(shards[5].astype(jnp.bfloat16), "ctx").astype(jnp.float32),
        lax.psum(shards[6].astype(jnp.bfloat16), "ctx").astype(jnp.float32),
        lax.psum(shards[7].astype(jnp.bfloat16), "ctx").astype(jnp.float32),
        lax.psum(shards[8].astype(jnp.bfloat16), "ctx").astype(jnp.float32),
        lax.psum(shards[9].astype(jnp.bfloat16), "ctx").astype(jnp.float32),
    )
    return (
        result[None],
        input_grad[None],
        summed[0],
        summed[1],
        summed[2],
        summed[3],
        summed[4],
        summed[5],
        summed[6],
        summed[7],
        summed[8],
        summed[9],
    )


def solution(mesh):
    return jax.shard_map(
        on_device,
        mesh=mesh,
        in_specs=(
            P("fsdp", "ctx", None),
            P("fsdp", "ctx", None),
            P("fsdp", None),
            P("fsdp"),
            P("fsdp", None),
            P("fsdp", None),
            P("fsdp", None),
            P("fsdp", None),
            P("fsdp", None),
            P("fsdp"),
            P(None, "fsdp"),
            P(None, "fsdp"),
            P("fsdp", None),
        ),
        out_specs=(
            P("fsdp", "ctx", None),
            P("fsdp", "ctx", None),
            P("fsdp"),
            P("fsdp", None),
            P("fsdp", None),
            P("fsdp", None),
            P("fsdp", None),
            P("fsdp", None),
            P("fsdp"),
            P(None, "fsdp"),
            P(None, "fsdp"),
            P("fsdp", None),
        ),
        check_vma=False,
    )
```

profile of v0, /device:TPU:0, one launch (start us, length us, event | category | flops | bytes accessed | tf_op | source)
XLA Modules:
  0.0 1036.9 jit_solution(728526672755502800)
XLA Ops:
  9.4 6.0 all-gather
  16.6 12.5 %all-gather.10.cloned.1.call-done = bf16[1024,512]{1,0:T(8,128)(2,1)} async-done(((bf16[256,512]{1,0:T(8,128)(2,1)}), bf16[1024,512]{1,0:T(8,128)(2,1)}) %all-gather.10.cloned.1.call-update) | async-done | bytes 1048592 | tf_op jit(solution)/shard_map/all_gather | solution.py:76
  29.0 2.6 convolution_convert_fusion.14
  34.9 5.1 all-gather.1
  40.0 10.9 %all_gather.38 = bf16[1024,256]{1,0:T(8,128)(2,1)} all-gather(bf16[256,256]{1,0:T(8,128)(2,1)S(1)} %copy-done.41), channel_id=1, replica_groups=mesh['ctx'=8,'fsdp'=4] {'fsdp'}, dimensions={0}, use_global_device_ids=true | all-gather | bytes 655360 | tf_op jit(solution)/shard_map/all_gather | solution.py:78
  50.9 7.3 all_gather.37
  58.2 2.5 convolution_convert_fusion.13
  60.9 2.1 convolution_convert_fusion.6
  63.0 2.9 copy.75
  65.9 42.2 %all-gather.12.cloned.1.call-done = bf16[2048,512]{1,0:T(8,128)(2,1)} async-done(((bf16[256,512]{1,0:T(8,128)(2,1)}), bf16[2048,512]{1,0:T(8,128)(2,1)}) %all-gather.12.cloned.1.call-update) | async-done | bytes 2097168 | tf_op jit(solution)/shard_map/all_gather | solution.py:140
  108.1 3.9 copy.70
  112.0 2.5 broadcast.245.clone
  114.5 10.8 %while.41 = (s32[]{:T(128)}, f32[2,8,256]{2,1,0:T(8,128)S(1)}, f32[2,8,256]{2,1,0:T(8,128)S(1)}, f32[2,8,256,256]{3,2,1,0:T(8,128)}, s32[]{:T(128)}, /*index=5*/...) while((s32[]{:T(128)}, f32[2,8,256]{2,1,0:T(8,128)S(1)}, ...), condition=%wide.region_6.7_spmd.clone, body=%wide.region_1.6_spmd.clone.sunk | while | flops 1089676544 | bytes 58203600 | solution.py:147
  114.5 10.4 %conditional.6 = ((f32[2,8,256]{2,1,0:T(8,128)S(1)}, f32[2,8,256]{2,1,0:T(8,128)S(1)}, f32[2,8,256,256]{3,2,1,0:T(8,128)})) conditional(s32[]{:T(128)} %convert_element_type.380, (f32[2,8,256]{2,1,0:T(8,128)S(1)}, f32[2,8,256]{2,1,0:T(8,128)S(1)}, f32[2,8,256,256]{3,2,1,0:T(8,128)}) %tuple.129, (s32[]{:T(128)}, s32[]{:T(128)}, s32[]{:T(128)}, ...), branch_computations={%region_2.2_spmd, %region_3.5_spmd} | conditional | flops 1089676544 | bytes 58202268 | solution.py:128
  115.8 2.8 fusion.4
  120.8 2.1 multiply_add_fusion
  122.9 2.0 copy-done.1
  125.2 5.9 copy.71
  131.1 2.7 fusion.44
  135.6 2.6 multiply_reduce_fusion.3
  139.3 36.1 %all-gather.18.cloned.1.call-done = bf16[1024,2816]{0,1:T(8,128)(2,1)} async-done(((bf16[1024,704]{0,1:T(8,128)(2,1)}), bf16[1024,2816]{0,1:T(8,128)(2,1)}) %all-gather.18.cloned.1.call-update) | async-done | bytes 5767184 | tf_op jit(solution)/shard_map/all_gather | solution.py:83
  175.4 5.9 fusion.79
  181.4 38.9 %all-gather.20.cloned.1.call-done = bf16[1024,2816]{0,1:T(8,128)(2,1)} async-done(((bf16[1024,704]{0,1:T(8,128)(2,1)}), bf16[1024,2816]{0,1:T(8,128)(2,1)}) %all-gather.20.cloned.1.call-update) | async-done | bytes 5767184 | tf_op jit(solution)/shard_map/all_gather | solution.py:84
  220.3 5.9 fusion.80
  226.2 39.1 %all-gather.22.cloned.1.call-done = bf16[2816,1024]{1,0:T(8,128)(2,1)} async-done(((bf16[704,1024]{1,0:T(8,128)(2,1)}), bf16[2816,1024]{1,0:T(8,128)(2,1)}) %all-gather.22.cloned.1.call-update) | async-done | bytes 5767184 | tf_op jit(solution)/shard_map/all_gather | solution.py:85
  265.3 8.2 multiply_convert_fusion
  273.5 5.4 fusion.81
  279.2 2.0 multiply_reduce_fusion.1
  284.7 2.0 copy.73
  288.6 3.7 multiply_reduce_fusion
  292.3 2.4 broadcast.245
  296.3 20.4 %while.42 = (s32[]{:T(128)}, f32[2,8,256,256]{3,2,1,0:T(8,128)}, bf16[2048,512]{0,1:T(8,128)(2,1)}, s32[]{:T(128)}, s32[]{:T(128)}, /*index=5*/s32[]{:T(128)}, s...) while((s32[]{:T(128)}, f32[2,8,256,256]{3,2,1,0:T(8,128)}, ...), condition=%wide.region_13.14_spmd.clone, body=%wide.region_10.13_spmd.clone.sunk | while | flops 2699625728 | bytes 97771040 | solution.py:246
  296.3 14.2 %conditional.7 = (f32[2,8,256,256]{3,2,1,0:T(8,128)}, bf16[256,512]{0,1:T(8,128)(2,1)S(1)}) conditional(s32[]{:T(128)} %convert_element_type.381, f32[2,8,256,256]{3,2,1,0:T(8,128)} %get-tuple-element.1157, (s32[]{:T(128)}, s32[]{:T(128)}, s32[]{:T(128)}, s32[]{:T(128)}, bf16[2048,512]{0,1:T(8,128)(2,1)}, ...), branch_computations={%region_11.11_spmd, %region_12.12_spmd} | conditional | flops 2699625728 | bytes 97245368 | solution.py:233
  297.5 2.8 fusion.78
  300.4 4.5 fusion.18
  318.3 4.3 fusion.42
  322.7 2.5 convert_element_type.249
  327.9 2.7 convolution_convert_fusion.9
  330.6 2.3 convolution_convert_fusion.11
  333.0 2.2 convolution_convert_fusion.4
  335.5 2.0 convolution_convert_fusion.3
  337.6 152.6 %reduce-scatter.10.cloned.1.call-done = bf16[256,512]{0,1:T(8,128)(2,1)} async-done(((bf16[2048,512]{0,1:T(8,128)(2,1)}), bf16[256,512]{0,1:T(8,128)(2,1)}) %reduce-scatter.10.cloned.1.call-update) | async-done | bytes 262160 | tf_op jit(solution)/shard_map/reduce_scatter | solution.py:251
  490.3 2.5 convolution_convert_fusion.7
  492.8 5.5 convolution_convert_fusion.2
  498.4 5.7 convolution_convert_fusion.1
  505.5 5.3 convolution_convert_fusion
  510.8 2.6 reduce-scatter.16.cloned.1.call-done
  513.4 24.2 %reduce-scatter.18.cloned.1.call-done = bf16[256,256]{1,0:T(8,128)(2,1)} async-done(((bf16[1024,256]{1,0:T(8,128)(2,1)}), bf16[256,256]{1,0:T(8,128)(2,1)}) %reduce-scatter.18.cloned.1.call-update) | async-done | bytes 131088 | tf_op jit(solution)/shard_map/reduce_scatter | solution.py:289
  537.6 34.6 %reduce-scatter.12.cloned.1.call-done = bf16[256,1024]{1,0:T(8,128)(2,1)} async-done(((bf16[1024,1024]{1,0:T(8,128)(2,1)}), bf16[256,1024]{1,0:T(8,128)(2,1)}) %reduce-scatter.12.cloned.1.call-update) | async-done | bytes 524304 | tf_op jit(solution)/shard_map/reduce_scatter | solution.py:280
  572.2 34.6 %reduce-scatter.20.cloned.1.call-done = bf16[256,1024]{1,0:T(8,128)(2,1)} async-done(((bf16[1024,1024]{1,0:T(8,128)(2,1)}), bf16[256,1024]{1,0:T(8,128)(2,1)}) %reduce-scatter.20.cloned.1.call-update) | async-done | bytes 524304 | tf_op jit(solution)/shard_map/reduce_scatter | solution.py:292
  606.8 28.0 %reduce-scatter.14.cloned.1.call-done = bf16[256,512]{1,0:T(8,128)(2,1)} async-done(((bf16[1024,512]{1,0:T(8,128)(2,1)}), bf16[256,512]{1,0:T(8,128)(2,1)}) %reduce-scatter.14.cloned.1.call-update) | async-done | bytes 262160 | tf_op jit(solution)/shard_map/reduce_scatter | solution.py:283
  634.8 57.5 %reduce-scatter.22.cloned.1.call-done = bf16[1024,704]{0,1:T(8,128)(2,1)} async-done(((bf16[1024,2816]{0,1:T(8,128)(2,1)}), bf16[1024,704]{0,1:T(8,128)(2,1)}) %reduce-scatter.22.cloned.1.call-update) | async-done | bytes 1441808 | tf_op jit(solution)/shard_map/reduce_scatter | solution.py:298
  692.3 57.3 %reduce-scatter.24.cloned.1.call-done = bf16[1024,704]{0,1:T(8,128)(2,1)} async-done(((bf16[1024,2816]{0,1:T(8,128)(2,1)}), bf16[1024,704]{0,1:T(8,128)(2,1)}) %reduce-scatter.24.cloned.1.call-update) | async-done | bytes 1441808 | tf_op jit(solution)/shard_map/reduce_scatter | solution.py:301
  749.6 57.5 %reduce-scatter.26.cloned.1.call-done = bf16[704,1024]{1,0:T(8,128)(2,1)} async-done(((bf16[2816,1024]{1,0:T(8,128)(2,1)}), bf16[704,1024]{1,0:T(8,128)(2,1)}) %reduce-scatter.26.cloned.1.call-update) | async-done | bytes 1441808 | tf_op jit(solution)/shard_map/reduce_scatter | solution.py:304
  808.9 2.5 fusion.82
  811.4 5.3 fusion.53
  817.5 6.1 all-reduce.4
  823.7 22.1 %all-reduce.2 = (bf16[256]{0:T(256)(128)(2,1)S(1)}, bf16[256]{0:T(256)(128)(2,1)S(1)}) all-reduce(bf16[256]{0:T(256)(128)(2,1)S(1)} %dynamic-slice.1, bf16[256]{0:T(256)(128)(2,1)S(1)} %dynamic-slice.3), channel_id=1, replica_groups=mesh['ctx'=8,'fsdp'=4] {'ctx'}, use_global_device_ids=true, to_apply=%region_18.19 | all-reduce | flops 512 | bytes 2048 | tf_op jit(solution)/shard_map/psum | solution.py:309
  848.2 167.7 %all-reduce.7.cloned.1.call-done = (bf16[256,1024]{1,0:T(8,128)(2,1)}, bf16[256,512]{1,0:T(8,128)(2,1)}, bf16[256,256]{1,0:T(8,128)(2,1)}, bf16[256,256]{1,0:T(8...) async-done(((bf16[256,1024]{1,0:T(8,128)(2,1)}, bf16[256,512]{1,0:T(8,128)(2,1)}, ...) | async-done | bytes 5898256 | tf_op jit(solution)/shard_map/psum | solution.py:310
  1015.9 2.3 convert_element_type.261
  1018.2 1.8 convert_element_type.263
  1024.3 1.9 convert_element_type.275
  1026.3 1.9 convert_element_type.277
  1028.2 1.9 convert_element_type.279
  (219 shorter events, 48.0 us)
Async XLA Ops:
  7.2 21.8 %all-gather.10.cloned.1.call-start = ((), (), s32[]{:S(2)}) async-start(), calls=%async_computation.9 | async-start | bytes 1310720 | tf_op jit(solution)/shard_map/all_gather | solution.py:76
  7.9 50.3 %all-gather.14.cloned.1.call-start = ((), (), s32[]{:S(2)}) async-start(), calls=%async_computation.11 | async-start | bytes 2621440 | tf_op jit(solution)/shard_map/all_gather | solution.py:75
  8.7 99.4 %all-gather.12.cloned.1.call-start = ((), (), s32[]{:S(2)}) async-start(), calls=%async_computation.10 | async-start | bytes 2359296 | tf_op jit(solution)/shard_map/all_gather | solution.py:140
  31.6 3.3 copy-start.44
  31.6 8.4 copy-start.41
  31.6 19.3 %copy-start.42 = (bf16[256,256]{1,0:T(8,128)(2,1)S(1)}, bf16[256,256]{1,0:T(8,128)(2,1)}, u32[]{:S(2)}) copy-start(bf16[256,256]{1,0:T(8,128)(2,1)} %param.27) | copy-start | bytes 393220
  31.6 104.0 %all-gather.16.cloned.1.call-start = ((), (), s32[]{:S(2)}) async-start(), calls=%async_computation.12 | async-start | bytes 2621440 | tf_op jit(solution)/shard_map/all_gather | solution.py:79
  32.2 26.0 %copy-start.8 = (bf16[1,256,1024]{2,1,0:T(8,128)(2,1)S(1)}, bf16[1,256,1024]{2,1,0:T(8,128)(2,1)}, u32[]{:S(2)}) copy-start(bf16[1,256,1024]{2,1,0:T(8,128)(2,1)} %param.21) | copy-start | bytes 1572868
  32.2 143.2 %all-gather.18.cloned.1.call-start = ((), (), s32[]{:S(2)}) async-start(), calls=%async_computation.13 | async-start | bytes 7208960 | tf_op jit(solution)/shard_map/all_gather | solution.py:83
  32.8 187.5 %all-gather.20.cloned.1.call-start = ((), (), s32[]{:S(2)}) async-start(), calls=%async_computation.14 | async-start | bytes 7208960 | tf_op jit(solution)/shard_map/all_gather | solution.py:84
  33.4 231.9 %all-gather.22.cloned.1.call-start = ((), (), s32[]{:S(2)}) async-start(), calls=%async_computation.15 | async-start | bytes 7208960 | tf_op jit(solution)/shard_map/all_gather | solution.py:85
  34.1 456.1 %reduce-scatter.10.cloned.1.call-start = ((), (), s32[]{:S(2)}) async-start(), calls=%async_computation.16 | async-start | bytes 2359296 | tf_op jit(solution)/shard_map/reduce_scatter | solution.py:251
  58.2 4.8 copy-start.22
  60.9 2.1 copy-start.28
  118.6 2.2 copy-start
  122.9 2.0 copy-start.1
  131.1 4.0 copy-start.24
  133.8 1.3 copy-start.5
  135.6 2.7 copy-start.20
  138.2 1.0 copy-start.11
  139.3 81.0 %copy-start.18 = (bf16[256,1024]{1,0:T(8,128)(2,1)}, bf16[256,1024]{1,0:T(8,128)(2,1)S(1)}, u32[]{:S(2)}) copy-start(bf16[256,1024]{1,0:T(8,128)(2,1)S(1)} %multiply_convert_fusion.3) | copy-start | bytes 1572868
  273.5 5.4 copy-start.34
  273.5 5.4 copy-start.33
  273.5 5.4 copy-start.12
  273.5 5.7 copy-start.43
  279.2 2.0 copy-start.32
  281.2 2.0 copy-start.14
  281.6 1.0 copy-start.9
  283.2 3.6 copy-start.25
  288.6 3.8 copy-start.15
  300.4 4.5 copy-start.2
  304.9 2.2 copy-start.4
  305.0 2.9 copy-start.16
  307.8 2.0 copy-start.3
  316.7 1.6 copy-start.17
  322.6 190.8 %reduce-scatter.16.cloned.1.call-start = ((), (), s32[]{:S(2)}) async-start(), calls=%async_computation.19 | async-start | bytes 655360 | tf_op jit(solution)/shard_map/reduce_scatter | solution.py:286
  322.7 3.8 copy-start.29
  325.2 1.3 copy-start.7
  325.2 2.7 copy-start.6
  327.8 2.8 copy-start.23
  327.8 209.8 %reduce-scatter.18.cloned.1.call-start = ((), (), s32[]{:S(2)}) async-start(), calls=%async_computation.20 | async-start | bytes 655360 | tf_op jit(solution)/shard_map/reduce_scatter | solution.py:289
  330.6 241.6 %reduce-scatter.12.cloned.1.call-start = ((), (), s32[]{:S(2)}) async-start(), calls=%async_computation.17 | async-start | bytes 2621440 | tf_op jit(solution)/shard_map/reduce_scatter | solution.py:280
  333.0 4.5 copy-start.26
  333.0 2.5 copy-start.10
  333.0 2.5 copy-start.21
  335.2 271.6 %reduce-scatter.20.cloned.1.call-start = ((), (), s32[]{:S(2)}) async-start(), calls=%async_computation.21 | async-start | bytes 2621440 | tf_op jit(solution)/shard_map/reduce_scatter | solution.py:292
  337.5 155.3 %copy-start.19 = (bf16[256,1024]{1,0:T(8,128)(2,1)S(1)}, bf16[256,1024]{1,0:T(8,128)(2,1)}, u32[]{:S(2)}) copy-start(bf16[256,1024]{1,0:T(8,128)(2,1)} %copy-done.18) | copy-start | bytes 1572868
  337.6 297.3 %reduce-scatter.14.cloned.1.call-start = ((), (), s32[]{:S(2)}) async-start(), calls=%async_computation.18 | async-start | bytes 1310720 | tf_op jit(solution)/shard_map/reduce_scatter | solution.py:283
  492.8 199.5 %reduce-scatter.22.cloned.1.call-start = ((), (), s32[]{:S(2)}) async-start(), calls=%async_computation.22 | async-start | bytes 7208960 | tf_op jit(solution)/shard_map/reduce_scatter | solution.py:298
  498.4 251.2 %reduce-scatter.24.cloned.1.call-start = ((), (), s32[]{:S(2)}) async-start(), calls=%async_computation.23 | async-start | bytes 7208960 | tf_op jit(solution)/shard_map/reduce_scatter | solution.py:301
  504.1 1.4 copy-start.30
  504.1 302.9 %reduce-scatter.26.cloned.1.call-start = ((), (), s32[]{:S(2)}) async-start(), calls=%async_computation.24 | async-start | bytes 7208960 | tf_op jit(solution)/shard_map/reduce_scatter | solution.py:304
  510.8 505.1 %all-reduce.7.cloned.1.call-start = ((), (), s32[]{:S(2)}) async-start(), calls=%async_computation.25 | async-start | bytes 11796480 | tf_op jit(solution)/shard_map/psum | solution.py:310
  807.0 0.7 copy-start.45
  807.0 1.9 copy-start.27
  807.1 4.3 copy-start.13
  808.9 2.5 copy-start.31
  811.4 5.3 copy-start.38
  811.4 5.3 copy-start.39
  1015.9 7.3 copy-start.40
  1015.9 8.4 copy-start.37
  1023.2 3.0 copy-start.36
  1026.3 1.9 copy-start.35
Sparse Core Ops, SparseCore 0:
  9.6 19.4 all-gather.9
  30.6 25.3 all-gather.13
  58.7 49.3 all-gather.11
  109.5 21.0 all-gather.15
  132.0 43.3 all-gather.17
  176.9 43.3 all-gather.19
  221.9 43.3 all-gather.21
  322.7 167.4 reduce-scatter.9
  492.7 20.6 reduce-scatter.15
  515.9 21.6 reduce-scatter.17
  540.7 31.4 reduce-scatter.11
  575.3 31.4 reduce-scatter.19
  609.9 24.8 reduce-scatter.13
  637.4 54.8 reduce-scatter.21
  694.7 54.8 reduce-scatter.23
  752.1 54.8 reduce-scatter.25
  811.5 204.3 all-reduce.6
where the time goes:
time: 1050 us; the launch traced here: 1040 us
  waiting for transfers between devices  789 us (75%)
  matrix products  94.2 us (9%)
  blocking collectives  57.4 us (5%)
  local copies, waits for them, and re-layouts  45.5 us (4%)
  other arithmetic  33 us (3%)
  between operations  16 us (2%)
    psum x1, waiting for transfers between devices, on_device(): lax.psum(shards[1].astype(jnp.bfloat16), 'ctx').astype(jnp.float32)  168 us
    reduce_scatter x1, waiting for transfers between devices, on_device(): lax.psum_scatter(lax.dynamic_slice_in_dim(padded, offset, row_count, 0).a...  153 us
    reduce_scatter x1, waiting for transfers between devices, on_device(): lax.psum_scatter(gate_w_grad.astype(jnp.bfloat16), 'fsdp', scatter_dimens...  57.5 us
    reduce_scatter x1, waiting for transfers between devices, on_device(): lax.psum_scatter(down_grad.astype(jnp.bfloat16), 'fsdp', scatter_dimensio...  57.5 us
    reduce_scatter x1, waiting for transfers between devices, on_device(): lax.psum_scatter(up_w_grad.astype(jnp.bfloat16), 'fsdp', scatter_dimensio...  57.3 us
    all_gather x1, waiting for transfers between devices, on_device(): group_latent = lax.all_gather(latent, 'ctx', axis=0, tiled=True)  42.2 us
    all_gather x1, waiting for transfers between devices, on_device(): lax.all_gather(w_down, 'fsdp', axis=0, tiled=True)  39.1 us
    all_gather x1, waiting for transfers between devices, on_device(): lax.all_gather(w_up, 'fsdp', axis=1, tiled=True)  38.9 us
  transfers between devices with their start and end apart: 17, of which 15 were waited for; matrix products, arithmetic and copies ran while one was open for 9% of the time, Pallas kernels for 0%

commit v1 on v0

--- a/solution.py
+++ b/solution.py
@@ -10,6 +10,24 @@
 SEQ_MAX = 4096
 EPS = 1e-06
 NEGATIVE = -1e30
+
+
+def collect(shard, axis, dim):
+    ways, here, step = (lax.axis_size(axis), lax.axis_index(axis), shard.shape[dim])
+    shape = [n * ways if d == dim else n for d, n in enumerate(shard.shape)]
+    full = lax.dynamic_update_slice_in_dim(
+        jnp.zeros(shape, shard.dtype), shard, here * step, axis=dim
+    )
+    going_up = going_down = shard
+    for far in range(1, ways // 2 + 1):
+        going_up = lax.ppermute(going_up, axis, [(d, (d + 1) % ways) for d in range(ways)])
+        full = lax.dynamic_update_slice_in_dim(full, going_up, (here - far) % ways * step, axis=dim)
+        if 2 * far < ways:
+            going_down = lax.ppermute(going_down, axis, [(d, (d - 1) % ways) for d in range(ways)])
+            full = lax.dynamic_update_slice_in_dim(
+                full, going_down, (here + far) % ways * step, axis=dim
+            )
+    return full
 
 
 def norm_scale(values):
@@ -81,7 +99,7 @@
     gain_two, gate_full, up_full, down_full = (
         lax.all_gather(norm2_gain, "fsdp", axis=0, tiled=True),
         lax.all_gather(w_gate, "fsdp", axis=1, tiled=True),
-        lax.all_gather(w_up, "fsdp", axis=1, tiled=True),
+        collect(w_up, "fsdp", 1),
         lax.all_gather(w_down, "fsdp", axis=0, tiled=True),
     )
     gain_one_f = gain_one.astype(jnp.float32)

time: 1050 us -> 1000 us (0.952)
  waiting for transfers between devices: 789 us -> 729 us
  local copies, waits for them, and re-layouts: 45.5 us -> 61.2 us
  matrix products: 94.2 us -> 82.3 us
    ppermute x0 -> x3, waiting for transfers between devices: none -> 42.9 us  [the longest x2 42.9 us: collect(): lax.ppermute(going_up, axis, [(d, (d + 1) % ways) for d in range(ways)])]
    all_gather x1, waiting for transfers between devices: 42.2 us -> 0.02 us  [on_device(): group_latent = lax.all_gather(latent, 'ctx', axis=0, tiled=True)]
    all_gather x1 -> x0, waiting for transfers between devices: 38.9 us -> none  [on_device(): lax.all_gather(w_up, 'fsdp', axis=1, tiled=True)]
    reduce_scatter x1, waiting for transfers between devices: 2.6 us -> 24.9 us  [on_device(): lax.psum_scatter(key_up_grad.astype(jnp.bfloat16), 'fsdp', scatter_dimens...]
    reduce_scatter x1, waiting for transfers between devices: 24.2 us -> 5.11 us  [on_device(): lax.psum_scatter(value_grad.astype(jnp.bfloat16), 'fsdp', scatter_dimensi...]
    all_gather x1, waiting for transfers between devices: 36.1 us -> 19.8 us  [on_device(): lax.all_gather(w_gate, 'fsdp', axis=1, tiled=True)]
    all_gather x1, blocking collectives: 5.07 us -> 18.8 us  [on_device(): lax.all_gather(norm2_gain, 'fsdp', axis=0, tiled=True)]
  transfers between devices with their start and end apart: 17 -> 19, of which waited for: 15 -> 14; matrix products, arithmetic and copies ran while one was open for 9% -> 10% of each run, Pallas kernels for 0% -> 0%
where the time goes in v1:
time: 1000 us; the launch traced here: 990 us
  waiting for transfers between devices  729 us (73%)
  matrix products  82.3 us (8%)
  blocking collectives  67.7 us (7%)
  local copies, waits for them, and re-layouts  61.2 us (6%)
  other arithmetic  30.6 us (3%)
  between operations  16 us (2%)
    psum x1, waiting for transfers between devices, on_device(): lax.psum(shards[1].astype(jnp.bfloat16), 'ctx').astype(jnp.float32)  168 us
    reduce_scatter x1, waiting for transfers between devices, on_device(): lax.psum_scatter(lax.dynamic_slice_in_dim(padded, offset, row_count, 0).a...  145 us
    reduce_scatter x1, waiting for transfers between devices, on_device(): lax.psum_scatter(gate_w_grad.astype(jnp.bfloat16), 'fsdp', scatter_dimens...  57.6 us
    reduce_scatter x1, waiting for transfers between devices, on_device(): lax.psum_scatter(down_grad.astype(jnp.bfloat16), 'fsdp', scatter_dimensio...  57.4 us
    reduce_scatter x1, waiting for transfers between devices, on_device(): lax.psum_scatter(up_w_grad.astype(jnp.bfloat16), 'fsdp', scatter_dimensio...  57.3 us
    ppermute x2, waiting for transfers between devices, collect(): lax.ppermute(going_up, axis, [(d, (d + 1) % ways) for d in range(ways)])  42.9 us
    all_gather x1, waiting for transfers between devices, on_device(): lax.all_gather(w_down, 'fsdp', axis=0, tiled=True)  38.9 us
    reduce_scatter x1, waiting for transfers between devices, on_device(): lax.psum_scatter(query_w_grad.astype(jnp.bfloat16), 'fsdp', scatter_dimen...  34.7 us
  transfers between devices with their start and end apart: 19, of which 14 were waited for; matrix products, arithmetic and copies ran while one was open for 10% of the time, Pallas kernels for 0%

profile of v1, /device:TPU:0, one launch (start us, length us, event | category | flops | bytes accessed | tf_op | source)
XLA Modules:
  0.0 990.1 jit_solution(9024557704117578664)
XLA Ops:
  9.4 6.0 all-gather
  16.6 12.4 %all-gather.9.cloned.1.call-done = bf16[1024,512]{1,0:T(8,128)(2,1)} async-done(((bf16[256,512]{1,0:T(8,128)(2,1)}), bf16[1024,512]{1,0:T(8,128)(2,1)}) %all-gather.9.cloned.1.call-update) | async-done | bytes 1048592 | tf_op jit(solution)/shard_map/all_gather | solution.py:94
  29.0 2.7 convolution_convert_fusion.14
  35.3 42.9 %collective-permute-done = bf16[1024,704]{0,1:T(8,128)(2,1)} collective-permute-done((bf16[1024,704]{0,1:T(8,128)(2,1)S(1)}, bf16[1024,704]{0,1:T(8,128)(2,1)}, u32[]{:S(2)}, u32[]{:S(2)}) %collective-permute-start) | collective-permute-done | bytes 1441824 | tf_op jit(solution)/shard_map/ppermute | solution.py:23
  78.9 18.8 %all-gather.1 = bf16[4,1,256]{2,1,0:T(2,128)(2,1)S(1)} all-gather(bf16[1,1,256]{2,1,0:T(2,128)(2,1)S(1)} %reshape.281), channel_id=1, replica_groups=mesh['ctx'=8,'fsdp'=4] {'fsdp'}, dimensions={0}, use_global_device_ids=true | all-gather | bytes 2560 | tf_op jit(solution)/shard_map/all_gather | solution.py:100
  97.8 3.2 broadcast_in_dim.88
  102.2 7.0 all_gather.34
  109.3 7.7 all_gather.35
  117.0 2.6 constant_dynamic-update-slice_fusion.3
  119.6 2.6 constant_dynamic-update-slice_fusion.2
  122.2 2.7 constant_dynamic-update-slice_fusion.1
  124.9 2.3 convolution_convert_fusion.13
  127.5 2.1 convolution_convert_fusion.6
  129.6 2.9 copy.75
  132.5 3.9 copy.70
  136.4 2.5 broadcast.248.clone
  138.9 10.8 %while.41 = (s32[]{:T(128)}, f32[2,8,256]{2,1,0:T(8,128)S(1)}, f32[2,8,256]{2,1,0:T(8,128)S(1)}, f32[2,8,256,256]{3,2,1,0:T(8,128)}, s32[]{:T(128)}, /*index=5*/...) while((s32[]{:T(128)}, f32[2,8,256]{2,1,0:T(8,128)S(1)}, ...), condition=%wide.region_6.7_spmd.clone, body=%wide.region_1.0_spmd.clone.sunk | while | flops 1089676544 | bytes 58203592 | solution.py:165
  138.9 10.4 %conditional.6 = ((f32[2,8,256]{2,1,0:T(8,128)S(1)}, f32[2,8,256]{2,1,0:T(8,128)S(1)}, f32[2,8,256,256]{3,2,1,0:T(8,128)})) conditional(s32[]{:T(128)} %convert_element_type.378, (f32[2,8,256]{2,1,0:T(8,128)S(1)}, f32[2,8,256]{2,1,0:T(8,128)S(1)}, f32[2,8,256,256]{3,2,1,0:T(8,128)}) %tuple.129, (s32[]{:T(128)}, s32[]{:T(128)}, s32[]{:T(128)}, ...), branch_computations={%region_2.2_spmd, %region_3.5_spmd} | conditional | flops 1089676544 | bytes 58202268 | solution.py:146
  140.3 2.7 fusion.4
  145.2 2.1 multiply_add_fusion
  147.3 2.0 copy-done.1
  149.7 6.2 copy.71
  155.9 2.7 fusion.44
  160.5 2.6 multiply_reduce_fusion.3
  164.2 19.8 %all-gather.17.cloned.1.call-done = bf16[1024,2816]{0,1:T(8,128)(2,1)} async-done(((bf16[1024,704]{0,1:T(8,128)(2,1)}), bf16[1024,2816]{0,1:T(8,128)(2,1)}) %all-gather.17.cloned.1.call-update) | async-done | bytes 5767184 | tf_op jit(solution)/shard_map/all_gather | solution.py:101
  184.0 5.9 fusion.79
  189.9 38.9 %all-gather.19.cloned.1.call-done = bf16[2816,1024]{1,0:T(8,128)(2,1)} async-done(((bf16[704,1024]{1,0:T(8,128)(2,1)}), bf16[2816,1024]{1,0:T(8,128)(2,1)}) %all-gather.19.cloned.1.call-update) | async-done | bytes 5767184 | tf_op jit(solution)/shard_map/all_gather | solution.py:103
  228.8 4.7 fusion.73
  233.5 6.6 multiply_convert_fusion
  242.2 4.6 multiply_reduce_fusion.1
  250.3 2.0 copy.73
  252.3 2.0 convolution_convert_fusion.5
  254.3 3.7 multiply_reduce_fusion
  258.0 2.5 broadcast.248
  262.1 17.3 %while.42 = (s32[]{:T(128)}, f32[2,8,256,256]{3,2,1,0:T(8,128)}, bf16[2048,512]{0,1:T(8,128)(2,1)}, s32[]{:T(128)}, s32[]{:T(128)}, /*index=5*/s32[]{:T(128)}, s...) while((s32[]{:T(128)}, f32[2,8,256,256]{3,2,1,0:T(8,128)}, ...), condition=%wide.region_13.14_spmd.clone, body=%wide.region_10.13_spmd.clone.sunk | while | flops 2699625728 | bytes 80993792 | solution.py:264
  262.1 11.2 %conditional.7 = (f32[2,8,256,256]{3,2,1,0:T(8,128)}, bf16[256,512]{0,1:T(8,128)(2,1)S(1)}) conditional(s32[]{:T(128)} %convert_element_type.379, f32[2,8,256,256]{3,2,1,0:T(8,128)} %get-tuple-element.1157, (s32[]{:T(128)}, s32[]{:T(128)}, s32[]{:T(128)}, s32[]{:T(128)}, bf16[2048,512]{0,1:T(8,128)(2,1)}, ...), branch_computations={%region_11.11_spmd, %region_12.12_spmd} | conditional | flops 2699625728 | bytes 80468128 | solution.py:251
  271.2 2.1 copy-done.3
  281.0 4.3 fusion.42
  285.4 2.6 convolution_convert_fusion.9
  288.0 2.5 convert_element_type.249
  291.9 3.4 convolution_convert_fusion.3
  295.6 1.8 convolution_convert_fusion.11
  298.2 2.2 convolution_convert_fusion.4
  300.5 144.5 %reduce-scatter.10.cloned.1.call-done = bf16[256,512]{0,1:T(8,128)(2,1)} async-done(((bf16[2048,512]{0,1:T(8,128)(2,1)}), bf16[256,512]{0,1:T(8,128)(2,1)}) %reduce-scatter.10.cloned.1.call-update) | async-done | bytes 262160 | tf_op jit(solution)/shard_map/reduce_scatter | solution.py:269
  445.0 2.5 convolution_convert_fusion.7
  447.6 4.2 convolution_convert_fusion.2
  453.1 4.1 convolution_convert_fusion.1
  458.7 4.3 convolution_convert_fusion
  463.1 5.1 reduce-scatter.18.cloned.1.call-done
  468.2 24.9 %reduce-scatter.16.cloned.1.call-done = bf16[256,256]{1,0:T(8,128)(2,1)} async-done(((bf16[1024,256]{1,0:T(8,128)(2,1)}), bf16[256,256]{1,0:T(8,128)(2,1)}) %reduce-scatter.16.cloned.1.call-update) | async-done | bytes 131088 | tf_op jit(solution)/shard_map/reduce_scatter | solution.py:304
  493.1 34.4 %reduce-scatter.20.cloned.1.call-done = bf16[256,1024]{1,0:T(8,128)(2,1)} async-done(((bf16[1024,1024]{1,0:T(8,128)(2,1)}), bf16[256,1024]{1,0:T(8,128)(2,1)}) %reduce-scatter.20.cloned.1.call-update) | async-done | bytes 524304 | tf_op jit(solution)/shard_map/reduce_scatter | solution.py:310
  527.5 34.7 %reduce-scatter.12.cloned.1.call-done = bf16[256,1024]{1,0:T(8,128)(2,1)} async-done(((bf16[1024,1024]{1,0:T(8,128)(2,1)}), bf16[256,1024]{1,0:T(8,128)(2,1)}) %reduce-scatter.12.cloned.1.call-update) | async-done | bytes 524304 | tf_op jit(solution)/shard_map/reduce_scatter | solution.py:298
  562.2 27.9 %reduce-scatter.14.cloned.1.call-done = bf16[256,512]{1,0:T(8,128)(2,1)} async-done(((bf16[1024,512]{1,0:T(8,128)(2,1)}), bf16[256,512]{1,0:T(8,128)(2,1)}) %reduce-scatter.14.cloned.1.call-update) | async-done | bytes 262160 | tf_op jit(solution)/shard_map/reduce_scatter | solution.py:301
  590.1 57.6 %reduce-scatter.22.cloned.1.call-done = bf16[1024,704]{0,1:T(8,128)(2,1)} async-done(((bf16[1024,2816]{0,1:T(8,128)(2,1)}), bf16[1024,704]{0,1:T(8,128)(2,1)}) %reduce-scatter.22.cloned.1.call-update) | async-done | bytes 1441808 | tf_op jit(solution)/shard_map/reduce_scatter | solution.py:316
  647.7 57.3 %reduce-scatter.24.cloned.1.call-done = bf16[1024,704]{0,1:T(8,128)(2,1)} async-done(((bf16[1024,2816]{0,1:T(8,128)(2,1)}), bf16[1024,704]{0,1:T(8,128)(2,1)}) %reduce-scatter.24.cloned.1.call-update) | async-done | bytes 1441808 | tf_op jit(solution)/shard_map/reduce_scatter | solution.py:319
  705.0 57.4 %reduce-scatter.26.cloned.1.call-done = bf16[704,1024]{1,0:T(8,128)(2,1)} async-done(((bf16[2816,1024]{1,0:T(8,128)(2,1)}), bf16[704,1024]{1,0:T(8,128)(2,1)}) %reduce-scatter.26.cloned.1.call-update) | async-done | bytes 1441808 | tf_op jit(solution)/shard_map/reduce_scatter | solution.py:322
  764.3 2.3 fusion.81
  766.7 5.6 fusion.53
  773.1 6.1 all-reduce.4
  779.3 22.1 %all-reduce.2 = (bf16[256]{0:T(256)(128)(2,1)S(1)}, bf16[256]{0:T(256)(128)(2,1)S(1)}) all-reduce(bf16[256]{0:T(256)(128)(2,1)S(1)} %dynamic-slice.1, bf16[256]{0:T(256)(128)(2,1)S(1)} %dynamic-slice.3), channel_id=1, replica_groups=mesh['ctx'=8,'fsdp'=4] {'ctx'}, use_global_device_ids=true, to_apply=%region_18.19 | all-reduce | flops 512 | bytes 2048 | tf_op jit(solution)/shard_map/psum | solution.py:327
  803.8 167.7 %all-reduce.7.cloned.1.call-done = (bf16[256,1024]{1,0:T(8,128)(2,1)}, bf16[256,512]{1,0:T(8,128)(2,1)}, bf16[256,256]{1,0:T(8,128)(2,1)}, bf16[256,256]{1,0:T(8...) async-done(((bf16[256,1024]{1,0:T(8,128)(2,1)}, bf16[256,512]{1,0:T(8,128)(2,1)}, ...) | async-done | bytes 5898256 | tf_op jit(solution)/shard_map/psum | solution.py:328
  971.5 3.4 convert_element_type.275
  974.9 1.9 convert_element_type.277
  976.9 1.9 convert_element_type.279
  (238 shorter events, 53.4 us)
Async XLA Ops:
  7.2 21.8 %all-gather.9.cloned.1.call-start = ((), (), s32[]{:S(2)}) async-start(), calls=%async_computation.9 | async-start | bytes 1310720 | tf_op jit(solution)/shard_map/all_gather | solution.py:94
  7.9 117.0 %all-gather.13.cloned.1.call-start = ((), (), s32[]{:S(2)}) async-start(), calls=%async_computation.11 | async-start | bytes 2621440 | tf_op jit(solution)/shard_map/all_gather | solution.py:93
  8.7 123.8 %all-gather.11.cloned.1.call-start = ((), (), s32[]{:S(2)}) async-start(), calls=%async_computation.10 | async-start | bytes 2359296 | tf_op jit(solution)/shard_map/all_gather | solution.py:158
  15.3 109.6 %copy-start.42 = (f32[4,1,256]{2,1,0:T(1,128)}, f32[4,1,256]{2,1,0:T(1,128)S(1)}, u32[]{:S(2)}) copy-start(f32[4,1,256]{2,1,0:T(1,128)S(1)} %convert_element_type.282) | copy-start | bytes 12292
  16.6 108.3 %copy-start.44 = (f32[256]{0:T(256)}, f32[256]{0:T(256)S(1)}, u32[]{:S(2)}) copy-start(f32[256]{0:T(256)S(1)} %add_rsqrt_fusion.1) | copy-start | bytes 3076
  29.0 4.5 copy-start.30
  29.0 49.9 %copy-start.46 = (bf16[256]{0:T(256)(128)(2,1)S(1)}, bf16[256]{0:T(256)(128)(2,1)}, u32[]{:S(2)}) copy-start(bf16[256]{0:T(256)(128)(2,1)} %param.30) | copy-start | bytes 1540
  31.7 128.7 %all-gather.15.cloned.1.call-start = ((), (), s32[]{:S(2)}) async-start(), calls=%async_computation.12 | async-start | bytes 2621440 | tf_op jit(solution)/shard_map/all_gather | solution.py:97
  32.3 151.6 %all-gather.17.cloned.1.call-start = ((), (), s32[]{:S(2)}) async-start(), calls=%async_computation.13 | async-start | bytes 7208960 | tf_op jit(solution)/shard_map/all_gather | solution.py:101
  32.9 195.9 %all-gather.19.cloned.1.call-start = ((), (), s32[]{:S(2)}) async-start(), calls=%async_computation.14 | async-start | bytes 7208960 | tf_op jit(solution)/shard_map/all_gather | solution.py:103
  33.5 411.5 %reduce-scatter.10.cloned.1.call-start = ((), (), s32[]{:S(2)}) async-start(), calls=%async_computation.15 | async-start | bytes 2359296 | tf_op jit(solution)/shard_map/reduce_scatter | solution.py:269
  33.5 44.7 %collective-permute-start = (bf16[1024,704]{0,1:T(8,128)(2,1)S(1)}, bf16[1024,704]{0,1:T(8,128)(2,1)}, u32[]{:S(2)}, u32[]{:S(2)}) collective-permute-start(bf16[1024,704]{0,1:T(8,128)(2,1)S(1)} %copy-done.30), channel_id=1, source_target_pairs={{0,1},{1,2},{2,3},{3,0},{4,5},{5,6},{6,7},{7,4},{8,9},{9,10},{10,1... | collective-permute-start | bytes 4325384 | tf_op jit(solution)/shard_map/ppermute | solution.py:23
  33.8 85.8 %collective-permute-start.1 = (bf16[1024,704]{0,1:T(8,128)(2,1)S(1)}, bf16[1024,704]{0,1:T(8,128)(2,1)}, u32[]{:S(2)}, u32[]{:S(2)}) collective-permute-start(bf16[1024,704]{0,1:T(8,128)(2,1)S(1)} %copy-done.30), channel_id=1, source_target_pairs={{0,3},{1,0},{2,1},{3,2},{4,7},{5,4},{6,5},{7,6},{8,11},{9,8},{10,9... | collective-permute-start | bytes 4325384 | tf_op jit(solution)/shard_map/ppermute | solution.py:26
  78.2 44.0 %collective-permute-start.2 = (bf16[1024,704]{0,1:T(8,128)(2,1)}, bf16[1024,704]{0,1:T(8,128)(2,1)}, u32[]{:S(2)}, u32[]{:S(2)}) collective-permute-start(bf16[1024,704]{0,1:T(8,128)(2,1)} %collective-permute-done), channel_id=1, source_target_pairs={{0,1},{1,2},{2,3},{3,0},{4,5},{5,6},{6,7},{7,4},{8,9},{9,10},{10,1... | collective-permute-start | bytes 4325384 | tf_op jit(solution)/shard_map/ppermute | solution.py:23
  100.9 8.3 copy-start.39
  109.3 18.2 %copy-start.17 = (bf16[1024,256]{1,0:T(8,128)(2,1)}, bf16[1024,256]{1,0:T(8,128)(2,1)S(1)}, u32[]{:S(2)}) copy-start(bf16[1024,256]{1,0:T(8,128)(2,1)S(1)} %all_gather.34) | copy-start | bytes 1572868
  119.6 5.3 copy-start.6
  127.5 2.1 copy-start.21
  143.0 2.2 copy-start
  147.3 2.0 copy-start.1
  155.9 4.0 copy-start.18
  160.4 2.7 copy-start.16
  228.8 4.7 copy-start.48
  228.8 11.3 %slice-start = ((s8[5767168]{0:T(1024)(128)(4,1)}), s8[4194304]{0:T(1024)(128)(4,1)S(1)}, s32[]{:S(2)}) async-start(s8[5767168]{0:T(1024)(128)(4,1)} %bitcast.216), calls=%async_computation.25 | async-start | bytes 8388608
  233.5 6.6 slice-start.1
  240.1 1.7 copy-start.28
  240.1 1.7 copy-start.26
  240.1 2.0 copy-start.10
  242.1 4.6 copy-start.24
  246.7 2.0 copy-start.12
  254.3 3.8 copy-start.13
  263.4 1.6 copy-start.14
  267.8 2.2 copy-start.2
  271.2 2.1 copy-start.3
  279.4 1.6 copy-start.15
  281.0 4.3 copy-start.5
  285.3 182.9 %reduce-scatter.18.cloned.1.call-start = ((), (), s32[]{:S(2)}) async-start(), calls=%async_computation.19 | async-start | bytes 655360 | tf_op jit(solution)/shard_map/reduce_scatter | solution.py:307
  288.0 205.1 %reduce-scatter.16.cloned.1.call-start = ((), (), s32[]{:S(2)}) async-start(), calls=%async_computation.18 | async-start | bytes 655360 | tf_op jit(solution)/shard_map/reduce_scatter | solution.py:304
  288.0 2.5 copy-start.22
  291.8 235.7 %reduce-scatter.20.cloned.1.call-start = ((), (), s32[]{:S(2)}) async-start(), calls=%async_computation.20 | async-start | bytes 2621440 | tf_op jit(solution)/shard_map/reduce_scatter | solution.py:310
  295.3 2.9 copy-start.43
  295.3 2.9 copy-start.45
  295.3 266.9 %reduce-scatter.12.cloned.1.call-start = ((), (), s32[]{:S(2)}) async-start(), calls=%async_computation.16 | async-start | bytes 2621440 | tf_op jit(solution)/shard_map/reduce_scatter | solution.py:298
  300.4 147.2 %copy-start.29 = (bf16[256,2816]{1,0:T(8,128)(2,1)S(1)}, bf16[256,2816]{1,0:T(8,128)(2,1)}, u32[]{:S(2)}) copy-start(bf16[256,2816]{1,0:T(8,128)(2,1)} %copy-done.28) | copy-start | bytes 4325380
  300.4 289.7 %reduce-scatter.14.cloned.1.call-start = ((), (), s32[]{:S(2)}) async-start(), calls=%async_computation.17 | async-start | bytes 1310720 | tf_op jit(solution)/shard_map/reduce_scatter | solution.py:301
  447.5 200.2 %reduce-scatter.22.cloned.1.call-start = ((), (), s32[]{:S(2)}) async-start(), calls=%async_computation.21 | async-start | bytes 7208960 | tf_op jit(solution)/shard_map/reduce_scatter | solution.py:316
  451.8 1.4 copy-start.27
  451.8 253.2 %reduce-scatter.24.cloned.1.call-start = ((), (), s32[]{:S(2)}) async-start(), calls=%async_computation.22 | async-start | bytes 7208960 | tf_op jit(solution)/shard_map/reduce_scatter | solution.py:319
  457.3 1.4 copy-start.23
  457.3 1.5 copy-start.25
  457.3 305.2 %reduce-scatter.26.cloned.1.call-start = ((), (), s32[]{:S(2)}) async-start(), calls=%async_computation.23 | async-start | bytes 7208960 | tf_op jit(solution)/shard_map/reduce_scatter | solution.py:322
  463.0 508.5 %all-reduce.7.cloned.1.call-start = ((), (), s32[]{:S(2)}) async-start(), calls=%async_computation.24 | async-start | bytes 11796480 | tf_op jit(solution)/shard_map/psum | solution.py:328
  762.4 1.9 copy-start.20
  762.5 4.2 copy-start.11
  766.7 5.6 copy-start.33
  766.7 5.6 copy-start.34
  772.4 30.2 %copy-start.8 = (f32[256,1024]{1,0:T(8,128)S(1)}, f32[256,1024]{1,0:T(8,128)}, u32[]{:S(2)}) copy-start(f32[256,1024]{1,0:T(8,128)} %copy-done.7) | copy-start | bytes 3145732
  971.5 3.4 copy-start.32
  974.9 1.9 copy-start.31
  976.9 2.0 copy-start.36
  976.9 3.0 copy-start.35
  976.9 4.1 copy-start.37
  978.8 3.0 copy-start.41
  978.8 3.8 copy-start.40
  (6 other events, 6.0 us)
Sparse Core Ops, SparseCore 0:
  9.6 19.4 all-gather.8
  30.6 33.9 all-gather.12
  67.3 49.2 all-gather.10
  118.0 21.0 all-gather.14
  140.5 43.3 all-gather.16
  185.4 43.3 all-gather.18
  285.4 159.5 reduce-scatter.9
  447.5 20.6 reduce-scatter.17
  471.4 21.6 reduce-scatter.15
  496.0 31.4 reduce-scatter.19
  530.8 31.4 reduce-scatter.11
  565.2 24.8 reduce-scatter.13
  592.8 54.8 reduce-scatter.21
  650.1 54.8 reduce-scatter.23
  707.5 54.8 reduce-scatter.25
  766.9 204.5 all-reduce.6
